TPU v7x, 256 devices: a whole 4x4x8 slice. The times are simulated.
256 devices in a mesh: req: 4 (over x), blk: 64 (over z, y, core).
Axes of the slice: x: 4, y: 4, z: 8, core: 2. Of those that a mesh axis runs over, the one named last changes fastest.
Arguments:
- tokens: bfloat16 [4, 8192, 2048], P('req', 'blk'), may hold values from -6 to 6
- block_ids: int32 [4, 128], P('req', 'blk'), may hold values from 0 to 127, as said below
- lengths: int32 [4], P('req'), may hold values from 4097 to 8192, as said below
- page_table: int32 [4, 2, 128], P('req'), may hold values from 0 to 255, as said below
- qkv_weight: bfloat16 [2048, 3072], P(('req', 'blk')), may hold values from -0.125 to 0.125
- q_gain: float32 [256], replicated
- k_gain: float32 [256], replicated
Outputs:
- attended: bfloat16 [4, 8192, 2048], P('req', 'blk')
- kv_cache: bfloat16 [4, 256, 64, 512], P('req', 'blk')
Inputs may be any that keep to these rules, and one draw needn't show every extreme that they name: `lengths`: one prompt has length exactly 8192. `block_ids`: the two entries of one device are b and 127 - b; over a prompt the first entries are a permutation of 0 to 63. `page_table`: each prompt's entries are a permutation of 0 to 255.
All inputs are finite; a program needn't handle non-finite values.
Results may differ from a plain program's by a relative error of at most 0.013.
The roundings to bfloat16 on the way count: a program that leaves them out, or rounds other values in their place, can miss the bound.
Values may be sent and summed in bfloat16 or wider, within the bound.
A program may use at most 128 MiB of HBM per device.

v0:
```python
import math
import jax
import jax.numpy as jnp
from jax import lax
from jax.sharding import PartitionSpec as P

H = 8
KVH = 2
HD = 256
ROPE_BASE = 1000000.0
NORM_EPS = 1e-06
FLOOR_SCORE = -1e30


def head_norm(tensor, scale_gain):
    return (
        tensor
        * lax.rsqrt(jnp.mean(tensor * tensor, axis=-1, keepdims=True) + NORM_EPS)
        * scale_gain
    )


def rotary(tensor, positions):
    half_dim = tensor.shape[-1] // 2
    channel = jnp.arange(half_dim).astype(jnp.float32)
    inverse = jnp.power(jnp.float32(ROPE_BASE), -2.0 * channel / tensor.shape[-1])
    angles = positions.astype(jnp.float32)[:, None] * inverse[None, :]
    cosine = jnp.cos(angles)[:, None, :]
    sine_part = jnp.sin(angles)[:, None, :]
    front_half = tensor[..., :half_dim]
    second = tensor[..., half_dim:]
    return jnp.concatenate(
        [front_half * cosine - second * sine_part, second * cosine + front_half * sine_part], -1
    )


def body(tokens, block_ids, lengths, page_table, qkv_weight, q_gain, k_gain):
    local_rows = tokens[0]
    row_count = local_rows.shape[0]
    blk_rows = row_count // 2
    groups = H // KVH
    projected = jnp.dot(
        local_rows,
        lax.all_gather(qkv_weight, ("req", "blk"), axis=0, tiled=True),
        preferred_element_type=jnp.float32,
    )
    own_ids = block_ids[0]
    positions = (
        own_ids[:, None] * blk_rows + jnp.arange(blk_rows, dtype=jnp.int32)[None, :]
    ).reshape(row_count)
    length = lengths[0]
    query_raw = projected[:, : H * HD].reshape(row_count, H, HD)
    key_raw = projected[:, H * HD : (H + KVH) * HD].reshape(row_count, KVH, HD)
    value_raw = projected[:, (H + KVH) * HD :].reshape(row_count, KVH, HD)
    queries = (
        rotary(head_norm(query_raw, q_gain), positions)
        .astype(jnp.bfloat16)
        .reshape(row_count, KVH, groups, HD)
    )
    send_keys = (
        rotary(head_norm(key_raw, k_gain), positions)
        .astype(jnp.bfloat16)
        .reshape(row_count, KVH * HD)
    )
    send_values = head_norm(value_raw, 1.0).astype(jnp.bfloat16).reshape(row_count, KVH * HD)
    all_ids = lax.all_gather(block_ids, "blk", axis=1, tiled=True)[0]
    table_size = all_ids.shape[0]
    slot_count = page_table.shape[1] * page_table.shape[2] // lax.axis_size("blk")
    my_slots = lax.axis_index("blk") * slot_count + jnp.arange(slot_count, dtype=jnp.int32)
    slot_match = page_table[0][None, :, :] == my_slots[:, None, None]
    head_grid = jnp.arange(page_table.shape[1], dtype=jnp.int32)[None, :, None]
    block_grid = jnp.arange(page_table.shape[2], dtype=jnp.int32)[None, None, :]
    slot_head = jnp.sum(jnp.where(slot_match, head_grid, 0), axis=(1, 2))
    slot_block = jnp.sum(jnp.where(slot_match, block_grid, 0), axis=(1, 2))
    query_live = positions < length
    running_max = jnp.full((row_count, KVH, groups), FLOOR_SCORE, jnp.float32)
    running_sum = jnp.zeros((row_count, KVH, groups), jnp.float32)
    weighted = jnp.zeros((row_count, KVH, groups, HD), jnp.float32)
    pages_out = jnp.zeros((slot_count, blk_rows, 2 * HD), jnp.bfloat16)
    piece_keys = lax.all_gather(send_keys, "blk", axis=0, tiled=True)
    piece_values = lax.all_gather(send_values, "blk", axis=0, tiled=True)
    piece_rows = piece_keys.shape[0]
    global_rows = jnp.arange(piece_rows, dtype=jnp.int32)
    block_index = global_rows // blk_rows
    lookup = jnp.sum(
        jnp.where(
            block_index[:, None] == jnp.arange(table_size, dtype=jnp.int32)[None, :],
            all_ids[None, :],
            0,
        ),
        1,
    )
    key_pos = lookup * blk_rows + global_rows % blk_rows
    key_heads = piece_keys.reshape(piece_rows, KVH, HD)
    value_heads = piece_values.reshape(piece_rows, KVH, HD)
    key_block = math.gcd(piece_rows, 512)

    def one_block(block_number, running):
        block_keys = lax.dynamic_slice_in_dim(key_heads, block_number * key_block, key_block, 0)
        block_values = lax.dynamic_slice_in_dim(value_heads, block_number * key_block, key_block, 0)
        block_pos = lax.dynamic_slice_in_dim(key_pos, block_number * key_block, key_block, 0)
        allowed = (block_pos[None, :] <= positions[:, None]) & (block_pos[None, :] < length)
        old_max, old_sum, old_weighted = running
        scores = jnp.einsum(
            "rgad,kgd->rgak", queries, block_keys, preferred_element_type=jnp.float32
        )
        mask_full = allowed[:, None, None, :]
        new_max = jnp.maximum(old_max, jnp.max(jnp.where(mask_full, scores, FLOOR_SCORE), -1))
        rescale = jnp.exp(old_max - new_max)
        weights = jnp.where(mask_full, jnp.exp(scores - new_max[..., None]), 0.0)
        new_sum = old_sum * rescale + jnp.sum(weights, -1)
        product = jnp.einsum(
            "rgak,kgd->rgad",
            weights.astype(jnp.bfloat16),
            block_values,
            preferred_element_type=jnp.float32,
        )
        return (new_max, new_sum, old_weighted * rescale[..., None] + product)

    running_max, running_sum, weighted = lax.fori_loop(
        0, piece_rows // key_block, one_block, (running_max, running_sum, weighted)
    )
    paired = jnp.concatenate([key_heads, value_heads], -1)
    row_numbers = jnp.arange(piece_rows, dtype=jnp.int32)
    page_offsets = jnp.arange(blk_rows, dtype=jnp.int32)
    page_list = []
    for slot_number in range(slot_count):
        target = slot_block[slot_number] * blk_rows
        is_start = key_pos == target
        present = jnp.any(is_start)
        first_row = jnp.sum(jnp.where(is_start, row_numbers, 0))
        rows_here = lax.dynamic_slice_in_dim(paired, first_row, blk_rows, 0)
        chosen = lax.dynamic_index_in_dim(rows_here, slot_head[slot_number], 1, keepdims=False)
        live_rows = target + page_offsets < length
        chosen = jnp.where(live_rows[:, None], chosen, jnp.zeros_like(chosen))
        page_list.append(jnp.where(present, chosen, pages_out[slot_number]))
    running_max, running_sum, weighted, pages_out = (
        running_max,
        running_sum,
        weighted,
        jnp.stack(page_list),
    )
    divisor = jnp.where(query_live[:, None, None], running_sum, 1.0)
    attended = jnp.where(query_live[:, None, None, None], weighted / divisor[..., None], 0.0)
    attended = attended.reshape(row_count, H * HD).astype(jnp.bfloat16)
    return (attended[None], pages_out[None])


def solution(mesh):
    in_specs = (
        P("req", "blk", None),
        P("req", "blk"),
        P("req"),
        P("req", None, None),
        P(("req", "blk"), None),
        P(),
        P(),
    )
    out_specs = (P("req", "blk", None), P("req", "blk", None, None))
    return jax.shard_map(body, mesh=mesh, in_specs=in_specs, out_specs=out_specs, check_vma=False)
```

profile of v0, /device:TPU:1, one launch (start us, length us, event | category | flops | bytes accessed | tf_op | source)
XLA Modules:
  0.0 402.0 jit_solution(17340536434207153513)
XLA Ops:
  8.0 128.9 %all-gather.4.cloned.1.call-done = bf16[2048,3072]{1,0:T(8,128)(2,1)} async-done(((bf16[8,3072]{1,0:T(8,128)(2,1)}), bf16[2048,3072]{1,0:T(8,128)(2,1)}) %all-gather.4.cloned.1.call-update) | async-done | bytes 12582928 | tf_op jit(solution)/shard_map/all_gather | solution.py:44
  136.8 6.4 %fusion.21 = f32[128,3072]{1,0:T(8,128)S(1)} fusion(bf16[2048,3072]{1,0:T(8,128)(2,1)} %all-gather.4.cloned.1.call-done, bf16[1,128,2048]{2,1,0:T(8,128)(2,1)S(1)} %copy-done), kind=kOutput, calls=%fused_computation.43 | convolution fusion | flops 1610612736 | bytes 14680064 | tf_op jit(solution)/shard_map/dot_general | solution.py:42
  146.1 0.8 copy.65
  147.2 0.7 fusion.48
  157.0 16.9 %all-reduce = s32[128]{0:T(128)S(1)} all-reduce(s32[128]{0:T(128)S(1)} %bitcast_dynamic-update-slice_fusion), channel_id=1, replica_groups=mesh['req'=4,'blk'=64] {'blk'}, use_global_device_ids=true, to_apply=%add | all-reduce | flops 128 | bytes 1024
  173.9 2.5 select_reduce_fusion
  178.8 0.7 fusion.45
  192.6 32.3 %all-gather.8.cloned.1.call-done = bf16[8192,512]{1,0:T(8,128)(2,1)} async-done(((bf16[128,512]{1,0:T(8,128)(2,1)}), bf16[8192,512]{1,0:T(8,128)(2,1)}) %all-gather.8.cloned.1.call-update) | async-done | bytes 8388624 | tf_op jit(solution)/shard_map/all_gather | solution.py:81
  224.9 11.3 %copy.84 = bf16[8192,512]{0,1:T(8,128)(2,1)} copy(bf16[8192,512]{1,0:T(8,128)(2,1)} %all-gather.8.cloned.1.call-done) | data formatting | bytes 16777216
  236.2 74.7 %all-gather.6.cloned.1.call-done = bf16[8192,512]{0,1:T(8,128)(2,1)} async-done(((bf16[128,512]{0,1:T(8,128)(2,1)}), bf16[8192,512]{0,1:T(8,128)(2,1)}) %all-gather.6.cloned.1.call-update) | async-done | bytes 8388624 | tf_op jit(solution)/shard_map/all_gather | solution.py:80
  310.9 1.7 fusion.24
  313.0 77.7 %while.18 = (s32[]{:T(128)}, f32[128,2,4]{0,2,1:T(4,128)S(1)}, f32[128,2,4]{0,2,1:T(4,128)S(1)}, f32[128,2,4,256]{0,3,2,1:T(8,128)S(1)}, s32[8192]{0:T(1024)S(1)...) while((s32[]{:T(128)}, f32[128,2,4]{0,2,1:T(4,128)S(1)}, ...), condition=%wide.region_7.8_spmd.clone, body=%wide.region_4.0_spmd.clone.sunk | while | flops 541988480 | bytes 10298591 | solution.py:120
  313.2 0.7 broadcast_compare_fusion.10
  314.1 1.6 fusion.62
  316.1 1.7 fusion.65
  318.1 0.7 broadcast_compare_fusion.10
  319.0 1.6 fusion.62
  321.0 1.7 fusion.65
  322.9 0.7 broadcast_compare_fusion.10
  323.9 1.6 fusion.62
  325.9 1.7 fusion.65
  327.8 0.7 broadcast_compare_fusion.10
  328.7 1.6 fusion.62
  330.7 1.7 fusion.65
  332.6 0.7 broadcast_compare_fusion.10
  333.6 1.6 fusion.62
  335.6 1.7 fusion.65
  337.5 0.7 broadcast_compare_fusion.10
  338.4 1.6 fusion.62
  340.4 1.7 fusion.65
  342.4 0.7 broadcast_compare_fusion.10
  343.3 1.6 fusion.62
  345.3 1.7 fusion.65
  347.2 0.7 broadcast_compare_fusion.10
  348.2 1.6 fusion.62
  350.2 1.7 fusion.65
  352.1 0.7 broadcast_compare_fusion.10
  353.0 1.6 fusion.62
  355.0 1.7 fusion.65
  356.9 0.7 broadcast_compare_fusion.10
  357.9 1.6 fusion.62
  359.9 1.7 fusion.65
  361.8 0.7 broadcast_compare_fusion.10
  362.7 1.6 fusion.62
  364.7 1.7 fusion.65
  366.7 0.7 broadcast_compare_fusion.10
  367.6 1.6 fusion.62
  369.6 1.7 fusion.65
  371.5 0.7 broadcast_compare_fusion.10
  372.4 1.6 fusion.62
  374.5 1.7 fusion.65
  376.4 0.7 broadcast_compare_fusion.10
  377.3 1.6 fusion.62
  379.3 1.7 fusion.65
  381.2 0.7 broadcast_compare_fusion.10
  382.2 1.6 fusion.62
  384.2 1.7 fusion.65
  386.1 0.7 broadcast_compare_fusion.10
  387.0 1.6 fusion.62
  389.0 1.7 fusion.65
  390.9 1.0 copy.83
  392.6 0.7 fusion.29
  393.9 0.8 fusion.27
  394.7 0.7 maximum_bitcast_fusion
  (187 shorter events, 23.3 us)
Async XLA Ops:
  7.2 129.7 %copy-start = (bf16[1,128,2048]{2,1,0:T(8,128)(2,1)S(1)}, bf16[1,128,2048]{2,1,0:T(8,128)(2,1)}, u32[]{:S(2)}) copy-start(bf16[1,128,2048]{2,1,0:T(8,128)(2,1)} %param.9) | copy-start | bytes 1572868
  7.2 129.6 %all-gather.4.cloned.1.call-start = ((), (), s32[]{:S(2)}) async-start(), calls=%async_computation | async-start | bytes 12632064 | tf_op jit(solution)/shard_map/all_gather | solution.py:44
  7.9 136.8 %copy-start.4 = (s32[1,2]{1,0:T(1,128)S(1)}, s32[1,2]{1,0:T(1,128)}, u32[]{:S(2)}) copy-start(s32[1,2]{1,0:T(1,128)} %param.10) | copy-start | bytes 28
  7.9 217.0 %all-gather.8.cloned.1.call-start = ((), (), s32[]{:S(2)}) async-start(), calls=%async_computation.2 | async-start | bytes 8519680 | tf_op jit(solution)/shard_map/all_gather | solution.py:81
  143.2 2.4 copy-start.1
  143.2 3.8 copy-start.3
  143.2 12.3 %copy-start.5 = (u32[256]{0:T(256)S(1)}, u32[256]{0:T(256)}, u32[]{:S(2)}) copy-start(u32[256]{0:T(256)} %constant.200) | copy-start | bytes 3076
  144.6 166.2 %all-gather.6.cloned.1.call-start = ((), (), s32[]{:S(2)}) async-start(), calls=%async_computation.1 | async-start | bytes 8519680 | tf_op jit(solution)/shard_map/all_gather | solution.py:80
  145.4 46.7 %copy-start.2 = (f32[256]{0:T(256)S(1)}, f32[256]{0:T(256)}, u32[]{:S(2)}) copy-start(f32[256]{0:T(256)} %param.14) | copy-start | bytes 3076
Sparse Core Ops, SparseCore 0:
  11.9 124.9 all-gather.3
  144.8 80.1 all-gather.7
  228.2 82.6 all-gather.5
where the time goes:
time: 404 us; the launch traced here: 402 us
  waiting for transfers between devices  237 us (59%)
  matrix products  59.4 us (15%)
  other arithmetic  37.3 us (9%)
  between operations  33 us (8%)
  local copies, waits for them, and re-layouts  17.7 us (4%)
  blocking collectives  16.9 us (4%)
    all_gather x1, waiting for transfers between devices, body(): lax.all_gather(qkv_weight, ('req', 'blk'), axis=0, tiled=True)  129 us
    all_gather x1, waiting for transfers between devices, body(): piece_keys = lax.all_gather(send_keys, 'blk', axis=0, tiled=True)  74.7 us
    all_gather x1, waiting for transfers between devices, body(): piece_values = lax.all_gather(send_values, 'blk', axis=0, tiled=True)  32.3 us
    dot_general x16, matrix products, one_block(): jnp.einsum('rgak,kgd->rgad', weights.astype(jnp.bfloat16), block_values,...  27.5 us
    dot_general x16, matrix products, one_block(): jnp.einsum('rgad,kgd->rgak', queries, block_keys, preferred_element_type=...  25.5 us
    unnamed x1, blocking collectives  16.9 us
    unnamed x18, local copies, waits for them, and re-layouts  12.4 us
    lt x16, other arithmetic, one_block(): block_pos[None, :] < length  11.6 us
  transfers between devices with their start and end apart: 3, of which 3 were waited for; matrix products, arithmetic and copies ran while one was open for 6% of the time, Pallas kernels for 0%

commit v1 on v0

--- a/solution.py
+++ b/solution.py
@@ -78,7 +78,9 @@
     weighted = jnp.zeros((row_count, KVH, groups, HD), jnp.float32)
     pages_out = jnp.zeros((slot_count, blk_rows, 2 * HD), jnp.bfloat16)
     piece_keys = lax.all_gather(send_keys, "blk", axis=0, tiled=True)
-    piece_values = lax.all_gather(send_values, "blk", axis=0, tiled=True)
+    piece_values = jnp.concatenate(
+        lax.all_to_all(jnp.stack([send_values] * lax.axis_size("blk")), "blk", 0, 0), axis=0
+    )
     piece_rows = piece_keys.shape[0]
     global_rows = jnp.arange(piece_rows, dtype=jnp.int32)
     block_index = global_rows // blk_rows

time: 404 us -> 510 us (1.26)
  blocking collectives: 16.9 us -> 202 us
  waiting for transfers between devices: 237 us -> 128 us
  local copies, waits for them, and re-layouts: 17.7 us -> 37 us
  starting transfers between devices: 0.12 us -> 8.05 us
    unnamed x1, blocking collectives: 16.9 us -> 202 us
    all_gather x1, waiting for transfers between devices: 74.7 us -> 0.01 us  [body(): piece_keys = lax.all_gather(send_keys, 'blk', axis=0, tiled=True)]
    all_gather x1 -> x0, waiting for transfers between devices: 32.3 us -> none  [body(): piece_values = lax.all_gather(send_values, 'blk', axis=0, tiled=True)]
    another operation x2 -> x4, local copies, waits for them, and re-layouts: 0.07 us -> 18.6 us  [the longest x1 13.3 us: body(): value_heads = piece_values.reshape(piece_rows, KVH, HD)]
    all_to_all x0 -> x1, local copies, waits for them, and re-layouts: none -> 12 us  [body(): lax.all_to_all(jnp.stack([send_values] * lax.axis_size('blk')), 'blk', 0, 0)]
    unnamed x18 -> x19, local copies, waits for them, and re-layouts: 12.4 us -> 1.08 us
    all_to_all x0 -> x1, starting transfers between devices: none -> 7.97 us  [body(): lax.all_to_all(jnp.stack([send_values] * lax.axis_size('blk')), 'blk', 0, 0)]
  transfers between devices with their start and end apart: 3 -> 3, of which waited for: 3 -> 1; matrix products, arithmetic and copies ran while one was open for 6% -> 7% of each run, Pallas kernels for 0% -> 0%
where the time goes in v1:
time: 510 us; the launch traced here: 506 us
  blocking collectives  202 us (40%)
  waiting for transfers between devices  128 us (25%)
  matrix products  59.4 us (12%)
  other arithmetic  37.2 us (7%)
  local copies, waits for them, and re-layouts  37 us (7%)
  between operations  32.7 us (6%)
  starting transfers between devices  8.05 us (2%)
    unnamed x1, blocking collectives  202 us
    all_gather x1, waiting for transfers between devices, body(): lax.all_gather(qkv_weight, ('req', 'blk'), axis=0, tiled=True)  128 us
    dot_general x16, matrix products, one_block(): jnp.einsum('rgak,kgd->rgad', weights.astype(jnp.bfloat16), block_values,...  27.5 us
    dot_general x16, matrix products, one_block(): jnp.einsum('rgad,kgd->rgak', queries, block_keys, preferred_element_type=...  25.5 us
    another operation x1, local copies, waits for them, and re-layouts, body(): value_heads = piece_values.reshape(piece_rows, KVH, HD)  13.3 us
    all_to_all x1, local copies, waits for them, and re-layouts, body(): lax.all_to_all(jnp.stack([send_values] * lax.axis_size('blk')), 'blk', 0, 0)  12 us
    lt x16, other arithmetic, one_block(): block_pos[None, :] < length  11.6 us
  transfers between devices with their start and end apart: 3, of which 1 were waited for; matrix products, arithmetic and copies ran while one was open for 7% of the time, Pallas kernels for 0%

profile of v1, /device:TPU:1, one launch (start us, length us, event | category | flops | bytes accessed | tf_op | source)
XLA Modules:
  0.0 505.9 jit_solution(5516919232190737044)
XLA Ops:
  9.1 127.8 %all-gather.3.cloned.1.call-done = bf16[2048,3072]{1,0:T(8,128)(2,1)} async-done(((bf16[8,3072]{1,0:T(8,128)(2,1)}), bf16[2048,3072]{1,0:T(8,128)(2,1)}) %all-gather.3.cloned.1.call-update) | async-done | bytes 12582928 | tf_op jit(solution)/shard_map/all_gather | solution.py:44
  136.8 6.4 %fusion.21 = f32[128,3072]{1,0:T(8,128)S(1)} fusion(bf16[2048,3072]{1,0:T(8,128)(2,1)} %all-gather.3.cloned.1.call-done, bf16[1,128,2048]{2,1,0:T(8,128)(2,1)S(1)} %copy-done), kind=kOutput, calls=%fused_computation.43 | convolution fusion | flops 1610612736 | bytes 14680064 | tf_op jit(solution)/shard_map/dot_general | solution.py:42
  144.5 5.2 %stack.4 = bf16[64,128,512]{1,2,0:T(8,128)(2,1)} broadcast(bf16[128,512]{0,1:T(8,128)(2,1)S(1)} %copy.86), dimensions={1,2} | broadcast | bytes 8519680 | tf_op jit(solution)/shard_map/stack | solution.py:82
  149.7 8.0 %all-to-all-start = ((bf16[64,128,512]{1,2,0:T(8,128)(2,1)}), bf16[64,128,512]{1,2,0:T(8,128)(2,1)}, u32[]{:S(2)}, u32[]{:S(2)}) async-start(bf16[64,128,512]{1,2,0:T(8,128)(2,1)} %stack.4), calls=%async_computation | async-start | bytes 16777216 | tf_op jit(solution)/shard_map/all_to_all | solution.py:82
  158.3 0.8 copy.79
  168.8 202.1 %all-reduce = s32[128]{0:T(128)S(1)} all-reduce(s32[128]{0:T(128)S(1)} %bitcast_dynamic-update-slice_fusion), channel_id=1, replica_groups=mesh['req'=4,'blk'=64] {'blk'}, use_global_device_ids=true, to_apply=%add | all-reduce | flops 128 | bytes 1024
  370.9 2.5 select_reduce_fusion
  375.9 0.7 fusion.45
  378.4 0.7 select_reduce_fusion.2
  389.2 12.0 %copy.87 = bf16[64,128,512]{1,0,2:T(8,128)(2,1)} copy(bf16[64,128,512]{1,2,0:T(8,128)(2,1)} %all-to-all-done) | data formatting | bytes 16777216 | tf_op jit(solution)/shard_map/all_to_all | solution.py:82
  401.2 13.3 %reshape_reshape.3 = bf16[8192,2,256]{0,2,1:T(8,128)(2,1)} reshape(bf16[64,128,512]{1,0,2:T(8,128)(2,1)} %copy.87) | data formatting | bytes 16777216 | tf_op jit(solution)/shard_map/reshape;reshape | solution.py:97
  414.5 77.8 %while.18 = (s32[]{:T(128)}, f32[128,2,4]{0,2,1:T(4,128)S(1)}, f32[128,2,4]{0,2,1:T(4,128)S(1)}, f32[128,2,4,256]{0,3,2,1:T(8,128)S(1)}, s32[8192]{0:T(1024)S(1)...) while((s32[]{:T(128)}, f32[128,2,4]{0,2,1:T(4,128)S(1)}, ...), condition=%wide.region_7.8_spmd.clone, body=%wide.region_4.0_spmd.clone.sunk | while | flops 541988480 | bytes 10298591 | solution.py:122
  414.7 0.7 broadcast_compare_fusion.10
  415.6 1.6 fusion.62
  417.6 1.7 fusion.65
  419.5 0.7 broadcast_compare_fusion.10
  420.5 1.6 fusion.62
  422.5 1.7 fusion.65
  424.4 0.7 broadcast_compare_fusion.10
  425.3 1.6 fusion.62
  427.4 1.7 fusion.65
  429.3 0.7 broadcast_compare_fusion.10
  430.2 1.6 fusion.62
  432.2 1.7 fusion.65
  434.1 0.7 broadcast_compare_fusion.10
  435.1 1.6 fusion.62
  437.1 1.7 fusion.65
  439.0 0.7 broadcast_compare_fusion.10
  439.9 1.6 fusion.62
  442.0 1.7 fusion.65
  443.9 0.7 broadcast_compare_fusion.10
  444.8 1.6 fusion.62
  446.8 1.7 fusion.65
  448.7 0.7 broadcast_compare_fusion.10
  449.7 1.6 fusion.62
  451.7 1.7 fusion.65
  453.6 0.7 broadcast_compare_fusion.10
  454.5 1.6 fusion.62
  456.5 1.7 fusion.65
  458.5 0.7 broadcast_compare_fusion.10
  459.4 1.6 fusion.62
  461.4 1.7 fusion.65
  463.3 0.7 broadcast_compare_fusion.10
  464.3 1.6 fusion.62
  466.3 1.7 fusion.65
  468.2 0.7 broadcast_compare_fusion.10
  469.1 1.6 fusion.62
  471.1 1.7 fusion.65
  473.1 0.7 broadcast_compare_fusion.10
  474.0 1.6 fusion.62
  476.0 1.7 fusion.65
  477.9 0.7 broadcast_compare_fusion.10
  478.9 1.6 fusion.62
  480.9 1.7 fusion.65
  482.8 0.7 broadcast_compare_fusion.10
  483.7 1.6 fusion.62
  485.7 1.7 fusion.65
  487.7 0.7 broadcast_compare_fusion.10
  488.6 1.6 fusion.62
  490.6 1.7 fusion.65
  492.5 1.0 copy.97
  493.5 1.8 fusion.24
  497.0 0.8 fusion.28
  498.4 0.7 maximum_bitcast_fusion
  (191 shorter events, 23.9 us)
Async XLA Ops:
  7.2 129.7 %copy-start = (bf16[1,128,2048]{2,1,0:T(8,128)(2,1)S(1)}, bf16[1,128,2048]{2,1,0:T(8,128)(2,1)}, u32[]{:S(2)}) copy-start(bf16[1,128,2048]{2,1,0:T(8,128)(2,1)} %param.9) | copy-start | bytes 1572868
  7.2 129.6 %all-gather.3.cloned.1.call-start = ((), (), s32[]{:S(2)}) async-start(), calls=%async_computation.1 | async-start | bytes 12632064 | tf_op jit(solution)/shard_map/all_gather | solution.py:44
  149.7 8.1 %copy-start.2 = (f32[256]{0:T(256)S(1)}, f32[256]{0:T(256)}, u32[]{:S(2)}) copy-start(f32[256]{0:T(256)} %param.15) | copy-start | bytes 3076
  149.7 9.4 %copy-start.4 = (s32[1,2,128]{2,1,0:T(2,128)S(1)}, s32[1,2,128]{2,1,0:T(2,128)}, u32[]{:S(2)}) copy-start(s32[1,2,128]{2,1,0:T(2,128)} %param.12) | copy-start | bytes 3076
  149.7 17.8 %copy-start.6 = (u32[256]{0:T(256)S(1)}, u32[256]{0:T(256)}, u32[]{:S(2)}) copy-start(u32[256]{0:T(256)} %constant.200) | copy-start | bytes 3076
  149.7 19.0 %copy-start.5 = (s32[1,2]{1,0:T(1,128)S(1)}, s32[1,2]{1,0:T(1,128)}, u32[]{:S(2)}) copy-start(s32[1,2]{1,0:T(1,128)} %param.10) | copy-start | bytes 28
  149.7 239.5 %all-to-all-start = ((bf16[64,128,512]{1,2,0:T(8,128)(2,1)}), bf16[64,128,512]{1,2,0:T(8,128)(2,1)}, u32[]{:S(2)}, u32[]{:S(2)}) async-start(bf16[64,128,512]{1,2,0:T(8,128)(2,1)} %stack.4), calls=%async_computation | async-start | bytes 16777216 | tf_op jit(solution)/shard_map/all_to_all | solution.py:82
  157.7 231.0 %copy-start.3 = (f32[256]{0:T(256)S(1)}, f32[256]{0:T(256)}, u32[]{:S(2)}) copy-start(f32[256]{0:T(256)} %param.14) | copy-start | bytes 3076
  157.7 256.8 %all-gather.5.cloned.1.call-start = ((), (), s32[]{:S(2)}) async-start(), calls=%async_computation.2 | async-start | bytes 8519680 | tf_op jit(solution)/shard_map/all_gather | solution.py:80
  493.5 5.6 %copy-start.1 = (bf16[1,128,2048]{2,1,0:T(8,128)(2,1)S(1)}, bf16[1,128,2048]{2,1,0:T(8,128)(2,1)}, u32[]{:S(2)}) copy-start(bf16[1,128,2048]{2,1,0:T(8,128)(2,1)} %param.9) | copy-start | bytes 1572868
Sparse Core Ops, SparseCore 0:
  11.9 124.9 all-gather.2
  161.8 183.5 all-gather.4
